TPU v7x, 512 devices: a whole 4x8x8 slice. The times are simulated.
512 devices in a mesh: traj: 4 (over x), slab: 128 (over z, y, core).
Axes of the slice: x: 4, y: 8, z: 8, core: 2. Of those that a mesh axis runs over, the one named last changes fastest.
Arguments:
- grad_out: bfloat16 [1024, 384, 128], P(('traj', 'slab')), parts along dimension 0, may hold values from -96 to 96
- cached: bfloat16 [1024, 384, 128], P('traj', 'slab'), parts along dimension 0, may hold values from -0.059814453 to 0.059814453
- values: bfloat16 [1024, 384, 128], P(('traj', 'slab')), parts along dimension 0, may hold values from -0.75 to 0.75
- query_x: bfloat16 [1024, 128], P('traj'), parts along dimension 0, may hold values from -6 to 6
- key_x: bfloat16 [1024, 128], P('traj'), parts along dimension 0, may hold values from -6 to 6
- query_y: bfloat16 [1536, 128], P('traj'), parts along dimension 0, may hold values from -6 to 6
- key_y: bfloat16 [1536, 128], P('traj'), parts along dimension 0, may hold values from -6 to 6
Outputs:
- grad_values: bfloat16 [1024, 384, 128], P(('traj', 'slab')), parts along dimension 0
- query_x_grad: float32 [1024, 128], P(('traj', 'slab')), parts along dimension 0
- key_x_grad: float32 [1024, 128], P(('traj', 'slab')), parts along dimension 0
- query_y_grad: float32 [1536, 128], P(('traj', 'slab')), parts along dimension 0
- key_y_grad: float32 [1536, 128], P(('traj', 'slab')), parts along dimension 0
There are 4 independent parts, one for each index of `traj`. A program takes and returns all parts, laid end to end along the dimension named above; each array names one. Nothing has to cross between parts.
All inputs are finite; a program needn't handle non-finite values.
Results may differ from a plain program's by a relative error of at most 0.0067.
Values may be sent and summed in bfloat16 or wider, within the bound.
No kernel may reach another device: no remote copies, remote signals or barrier semaphores. Data moves between devices by JAX's collectives and lax.ppermute only.
A program may use at most 64 MiB of HBM per device.

v0:
```python
import math

import jax
import jax.numpy as jnp
from jax import lax
from jax.sharding import PartitionSpec as P

HEADS = 4
HEAD = 32


def axis_kernel(queries, key_rows):
    scores = jnp.dot(queries, key_rows.T, preferred_element_type=jnp.float32) / math.sqrt(HEAD)
    return jax.nn.softmax(scores, axis=1)


def local_terms(kernel, coupling, queries, key_rows):
    row_delta = jnp.sum(kernel * coupling, axis=1)
    weighted = kernel * coupling
    grad_query = jnp.dot(
        weighted, key_rows.astype(jnp.float32), precision=lax.Precision.HIGHEST
    ) / math.sqrt(HEAD)
    grad_key = jnp.dot(
        weighted.T, queries.astype(jnp.float32), precision=lax.Precision.HIGHEST
    ) / math.sqrt(HEAD)
    return (grad_query, grad_key, row_delta)


def corrections(own_rows, own_cols, delta_total, queries, key_rows, start, count):
    own_delta = lax.dynamic_slice_in_dim(delta_total, start, count, 0)
    query_fix = (
        own_delta[:, None]
        * jnp.dot(own_rows, key_rows.astype(jnp.float32), precision=lax.Precision.HIGHEST)
        / math.sqrt(HEAD)
    )
    key_fix = jnp.dot(
        own_cols.T,
        delta_total[:, None] * queries.astype(jnp.float32),
        precision=lax.Precision.HIGHEST,
    ) / math.sqrt(HEAD)
    return (query_fix, key_fix)


def on_device(grad_out, cached, values, query_x, key_x, query_y, key_y):
    index = lax.axis_index("slab")
    x_rows = grad_out.shape[0]
    x_count = cached.shape[0]
    y_rows = cached.shape[1]
    x_start = index * x_rows
    y_start = index * y_rows
    grad_columns = lax.all_to_all(grad_out, "slab", split_axis=1, concat_axis=0, tiled=True)
    mixed_heads = []
    query_terms = []
    key_terms = []
    delta_terms = []
    row_slices = []
    col_slices = []
    for head_index in range(HEADS):
        offset = head_index * HEAD
        head_query = query_x[:, offset : offset + HEAD]
        head_key = key_x[:, offset : offset + HEAD]
        kernel = axis_kernel(head_query, head_key)
        grad_rows = grad_columns[:, :, offset : offset + HEAD].reshape(x_count, y_rows * HEAD)
        saved_rows = cached[:, :, offset : offset + HEAD].reshape(x_count, y_rows * HEAD)
        grad_mixed = lax.dot_general(
            kernel.astype(jnp.bfloat16),
            grad_rows,
            (((0,), (0,)), ((), ())),
            preferred_element_type=jnp.float32,
        ).astype(jnp.bfloat16)
        coupling = lax.dot_general(
            grad_rows, saved_rows, (((1,), (1,)), ((), ())), preferred_element_type=jnp.float32
        )
        grad_query, grad_key, row_delta = local_terms(kernel, coupling, head_query, head_key)
        query_terms.append(grad_query)
        key_terms.append(grad_key)
        delta_terms.append(row_delta)
        row_slices.append(lax.dynamic_slice_in_dim(kernel, x_start, x_rows, 0))
        col_slices.append(lax.dynamic_slice_in_dim(kernel, x_start, x_rows, 1))
        mixed_heads.append(grad_mixed.reshape(x_count, y_rows, HEAD))
    mixed_rows = lax.all_to_all(
        jnp.concatenate(mixed_heads, axis=2), "slab", split_axis=0, concat_axis=1, tiled=True
    )
    x_delta_total = lax.psum(jnp.stack(delta_terms), "slab")
    query_x_grad, key_x_grad = (
        lax.psum_scatter(
            jnp.concatenate(query_terms, axis=1), "slab", scatter_dimension=0, tiled=True
        ),
        lax.psum_scatter(
            jnp.concatenate(key_terms, axis=1), "slab", scatter_dimension=0, tiled=True
        ),
    )
    query_fixes = []
    key_fixes = []
    for head_index in range(HEADS):
        offset = head_index * HEAD
        query_fix, key_fix = corrections(
            row_slices[head_index],
            col_slices[head_index],
            x_delta_total[head_index],
            query_x[:, offset : offset + HEAD],
            key_x[:, offset : offset + HEAD],
            x_start,
            x_rows,
        )
        query_fixes.append(query_fix)
        key_fixes.append(key_fix)
    query_x_grad = query_x_grad - jnp.concatenate(query_fixes, axis=1)
    key_x_grad = key_x_grad - jnp.concatenate(key_fixes, axis=1)
    value_heads = []
    query_terms = []
    key_terms = []
    delta_terms = []
    row_slices = []
    col_slices = []
    for head_index in range(HEADS):
        offset = head_index * HEAD
        head_query = query_y[:, offset : offset + HEAD]
        head_key = key_y[:, offset : offset + HEAD]
        kernel = axis_kernel(head_query, head_key)
        mixed_head = mixed_rows[:, :, offset : offset + HEAD]
        value_head = values[:, :, offset : offset + HEAD]
        grad_value = jnp.einsum(
            "jk,xje->xke",
            kernel.astype(jnp.bfloat16),
            mixed_head,
            preferred_element_type=jnp.float32,
        )
        coupling = jnp.einsum(
            "xje,xke->jk", mixed_head, value_head, preferred_element_type=jnp.float32
        )
        grad_query, grad_key, row_delta = local_terms(kernel, coupling, head_query, head_key)
        query_terms.append(grad_query)
        key_terms.append(grad_key)
        delta_terms.append(row_delta)
        row_slices.append(lax.dynamic_slice_in_dim(kernel, y_start, y_rows, 0))
        col_slices.append(lax.dynamic_slice_in_dim(kernel, y_start, y_rows, 1))
        value_heads.append(grad_value.astype(jnp.bfloat16))
    y_delta_total = lax.psum(jnp.stack(delta_terms), "slab")
    query_y_grad, key_y_grad = (
        lax.psum_scatter(
            jnp.concatenate(query_terms, axis=1), "slab", scatter_dimension=0, tiled=True
        ),
        lax.psum_scatter(
            jnp.concatenate(key_terms, axis=1), "slab", scatter_dimension=0, tiled=True
        ),
    )
    query_fixes = []
    key_fixes = []
    for head_index in range(HEADS):
        offset = head_index * HEAD
        query_fix, key_fix = corrections(
            row_slices[head_index],
            col_slices[head_index],
            y_delta_total[head_index],
            query_y[:, offset : offset + HEAD],
            key_y[:, offset : offset + HEAD],
            y_start,
            y_rows,
        )
        query_fixes.append(query_fix)
        key_fixes.append(key_fix)
    query_y_grad = query_y_grad - jnp.concatenate(query_fixes, axis=1)
    key_y_grad = key_y_grad - jnp.concatenate(key_fixes, axis=1)
    grad_values = jnp.concatenate(value_heads, axis=2)
    return (grad_values, query_x_grad, key_x_grad, query_y_grad, key_y_grad)


def solution(mesh):
    return jax.shard_map(
        on_device,
        mesh=mesh,
        in_specs=(
            P(("traj", "slab"), None, None),
            P("traj", "slab", None),
            P(("traj", "slab"), None, None),
            P("traj", None),
            P("traj", None),
            P("traj", None),
            P("traj", None),
        ),
        out_specs=(
            P(("traj", "slab"), None, None),
            P(("traj", "slab"), None),
            P(("traj", "slab"), None),
            P(("traj", "slab"), None),
            P(("traj", "slab"), None),
        ),
        check_vma=False,
    )
```

profile of v0, /device:TPU:1, one launch (start us, length us, event | category | flops | bytes accessed | tf_op | source)
XLA Modules:
  0.0 824.5 jit_solution(5174410356687245763)
XLA Ops:
  7.2 1.8 copy.95
  9.0 19.0 %all-to-all-start = ((bf16[2,384,128]{2,0,1:T(2,128)(2,1)}), bf16[2,384,128]{2,0,1:T(2,128)(2,1)}, u32[]{:S(2)}, u32[]{:S(2)}) async-start(bf16[2,384,128]{2,0,1:T(2,128)(2,1)} %copy.95), calls=%async_computation | async-start | bytes 393216 | tf_op jit(solution)/shard_map/all_to_all | solution.py:51
  28.0 1.0 fusion.169
  31.7 1.3 dynamic-slice.8
  34.3 1.1 fusion.39
  35.4 0.7 fusion.38
  36.2 0.7 fusion.36
  37.1 0.7 fusion.40
  38.8 2.8 all-to-all-done
  41.6 1.1 copy.96
  42.7 1.8 fusion.177
  44.9 0.9 convolution_multiply_fusion.22
  45.8 0.8 fusion.178
  46.7 0.9 convolution_multiply_fusion.19
  47.5 0.8 convolution_multiply_fusion.23
  48.4 0.9 fusion.175
  49.3 0.9 convolution_multiply_fusion.16
  50.2 0.9 convolution_multiply_fusion.20
  51.1 1.0 fusion.165
  52.2 0.9 fusion.176
  53.1 0.7 copy-done.14
  53.8 0.9 convolution_multiply_fusion.21
  54.7 1.7 copy.148
  56.3 1.0 convolution_convert_fusion.7
  57.3 1.7 copy.150
  59.0 1.8 convolution_convert_fusion.5
  60.7 1.7 copy.149
  62.4 1.6 convolution_convert_fusion.6
  64.0 1.7 copy.151
  65.7 1.6 convolution_convert_fusion.4
  67.3 1.7 copy.104
  68.9 1.7 copy.102
  70.6 1.7 copy.103
  72.3 0.9 copy.101
  73.2 2.7 pad_maximum_fusion
  75.9 11.5 %all-to-all-start.1 = ((bf16[256,3,128]{2,1,0:T(4,128)(2,1)}), bf16[256,3,128]{2,1,0:T(4,128)(2,1)}, u32[]{:S(2)}, u32[]{:S(2)}) async-start(bf16[256,3,128]{2,1,0:T(4,128)(2,1)} %pad_maximum_fusion), calls=%async_computation.1 | async-start | bytes 524288 | tf_op jit(solution)/shard_map/all_to_all | solution.py:81
  87.7 1.5 pad_maximum_fusion.4
  91.9 10.4 %all-to-all-done.1 = bf16[256,3,128]{2,1,0:T(4,128)(2,1)} async-done(((bf16[256,3,128]{2,1,0:T(4,128)(2,1)}), bf16[256,3,128]{2,1,0:T(4,128)(2,1)}, u32[]{:S(2)}, u32[]{:S(2)}) %all-to-all-start.1) | async-done | bytes 196640 | tf_op jit(solution)/shard_map/all_to_all | solution.py:81
  102.3 1.0 copy.105
  103.4 1.5 fusion.164
  105.0 1.1 copy.153
  106.1 0.9 fusion.9
  107.4 1.1 convolution_multiply_fusion.10
  108.5 1.0 convolution_multiply_fusion.14
  109.5 1.1 copy.152
  110.6 0.8 fusion.8
  111.8 1.1 convolution_multiply_fusion.11
  112.9 1.0 convolution_multiply_fusion.15
  113.9 1.1 copy.155
  114.9 0.9 fusion.11
  116.3 1.1 convolution_multiply_fusion.8
  117.4 1.0 convolution_multiply_fusion.12
  118.4 1.1 copy.154
  119.7 0.7 copy-done.12
  121.3 1.0 convolution_multiply_fusion.13
  122.4 0.7 pad_maximum_fusion.1
  123.1 1.7 copy.127
  124.8 0.7 copy-done.31
  125.5 485.9 %all-reduce.4 = (f32[4,256]{1,0:T(4,128)S(1)}, f32[4,384]{1,0:T(4,128)S(1)}) all-reduce(f32[4,256]{1,0:T(4,128)S(1)} %copy-done.31, f32[4,384]{1,0:T(4,128)S(1)} %pad_maximum_fusion.6), channel_id=1, replica_groups=mesh['traj'=4,'slab'=128] {'slab'}, use_global_device_ids=true, to_apply=%region_21.0 | all-reduce | flops 2560 | bytes 20480 | tf_op jit(solution)/shard_map/psum | solution.py:84
  611.7 0.8 convolution_multiply_fusion.35
  618.9 0.7 pad_maximum_fusion.2
  619.8 0.7 pad_maximum_fusion.3
  621.4 192.3 %all-reduce.8.cloned.1.call-done = (f32[256,128]{0,1:T(8,128)}, f32[256,128]{0,1:T(8,128)}, f32[384,128]{0,1:T(8,128)}, f32[384,128]{0,1:T(8,128)}) async-done(((f32[256,128]{0,1:T(8,128)}, f32[256,128]{0,1:T(8,128)}, f32[384,128]{0,1:T(8,128)}, f32[384,128]{0,1:T(8,128)}), (f32[256,128]{0,1:T(8,128)}, f32[256,128]{0,1:T(8,128)}, f32[384,128]{0,1:T(8,128)}, ...) | async-done | bytes 655376
  813.6 1.1 dynamic-slice_subtract_fusion
  (145 shorter events, 20.5 us)
Async XLA Ops:
  9.0 19.0 %copy-start.1 = (bf16[256,128]{1,0:T(8,128)(2,1)S(1)}, bf16[256,128]{1,0:T(8,128)(2,1)}, u32[]{:S(2)}) copy-start(bf16[256,128]{1,0:T(8,128)(2,1)} %param.11) | copy-start | bytes 196612
  9.0 19.0 %copy-start.3 = (bf16[256,128]{1,0:T(8,128)(2,1)S(1)}, bf16[256,128]{1,0:T(8,128)(2,1)}, u32[]{:S(2)}) copy-start(bf16[256,128]{1,0:T(8,128)(2,1)} %param.10) | copy-start | bytes 196612
  9.0 32.6 %all-to-all-start = ((bf16[2,384,128]{2,0,1:T(2,128)(2,1)}), bf16[2,384,128]{2,0,1:T(2,128)(2,1)}, u32[]{:S(2)}, u32[]{:S(2)}) async-start(bf16[2,384,128]{2,0,1:T(2,128)(2,1)} %copy.95), calls=%async_computation | async-start | bytes 393216 | tf_op jit(solution)/shard_map/all_to_all | solution.py:51
  29.4 0.9 copy-start
  29.5 0.9 copy-start.2
  34.3 1.1 copy-start.13
  38.8 3.9 copy-start.4
  44.5 1.2 copy-start.8
  44.9 1.0 copy-start.5
  51.1 1.0 copy-start.6
  53.1 0.7 copy-start.14
  75.9 11.8 %copy-start.28 = (f32[256,32]{0,1:T(8,128)S(1)}, f32[256,32]{0,1:T(8,128)}, u32[]{:S(2)}) copy-start(f32[256,32]{0,1:T(8,128)} %convolution_multiply_fusion.22) | copy-start | bytes 98308
  75.9 26.4 %all-to-all-start.1 = ((bf16[256,3,128]{2,1,0:T(4,128)(2,1)}), bf16[256,3,128]{2,1,0:T(4,128)(2,1)}, u32[]{:S(2)}, u32[]{:S(2)}) async-start(bf16[256,3,128]{2,1,0:T(4,128)(2,1)} %pad_maximum_fusion), calls=%async_computation.1 | async-start | bytes 524288 | tf_op jit(solution)/shard_map/all_to_all | solution.py:81
  87.4 726.2 %all-reduce.8.cloned.1.call-start = ((), (), s32[]{:S(2)}) async-start(), calls=%async_computation.2 | async-start | bytes 1310720
  87.7 1.5 copy-start.33
  87.7 1.5 copy-start.34
  87.7 1.5 copy-start.35
  87.7 2.8 copy-start.15
  89.2 0.7 copy-start.32
  90.5 0.8 copy-start.26
  90.5 0.8 copy-start.27
  106.0 0.9 copy-start.9
  110.6 0.9 copy-start.10
  114.9 0.9 copy-start.11
  119.4 0.9 copy-start.12
  121.3 1.1 copy-start.23
  121.3 1.1 copy-start.24
  121.3 1.1 copy-start.25
  124.8 0.7 copy-start.31
  611.6 1.6 copy-start.7
  617.7 0.8 copy-start.21
  617.7 0.8 copy-start.22
  617.9 0.8 copy-start.19
  618.1 0.8 copy-start.17
  618.9 0.8 copy-start.16
  618.9 0.8 copy-start.18
  618.9 0.9 copy-start.20
  620.5 0.7 copy-start.36
  814.7 1.3 copy-start.30
  816.0 0.9 copy-start.29
Sparse Core Ops, SparseCore 0:
  620.6 192.9 all-reduce.7
where the time goes:
time: 827 us; the launch traced here: 825 us
  blocking collectives  486 us (59%)
  waiting for transfers between devices  206 us (25%)
  matrix products  37.6 us (5%)
  local copies, waits for them, and re-layouts  35.5 us (4%)
  starting transfers between devices  30.7 us (4%)
  between operations  15.8 us (2%)
  other arithmetic  13.5 us (2%)
    psum x1, blocking collectives, on_device(): x_delta_total = lax.psum(jnp.stack(delta_terms), 'slab')  486 us
    unnamed x2, waiting for transfers between devices  192 us
    unnamed x90, local copies, waits for them, and re-layouts  24.8 us
    all_to_all x1, starting transfers between devices, on_device(): lax.all_to_all(grad_out, 'slab', split_axis=1, concat_axis=0, tiled=True)  19 us
  transfers between devices with their start and end apart: 3, of which 3 were waited for; matrix products, arithmetic and copies ran while one was open for 1% of the time, Pallas kernels for 0%

commit v1 on v0

v1 whole, which is shorter than its diff:
```python
import functools
import math

import jax
import jax.numpy as jnp
from jax import lax
from jax.experimental import pallas as pl
from jax.experimental.pallas import tpu as pltpu
from jax.sharding import PartitionSpec as P

HEAD = 32
LANES = 128
XR = 2
YU = 3
TILES = XR * YU
SEND = 3 * TILES
BACK = TILES + 4
F32 = jnp.float32
BF16 = jnp.bfloat16
ROOT = math.sqrt(HEAD)


def dot(a, b, dims=((1,), (0,))):
    return lax.dot_general(a, b, (dims, ((), ())), preferred_element_type=F32)


def pack_kernel(grad_ref, cached_ref, values_ref, out_ref, rows_ref, send_ref):
    for part, ref in enumerate((grad_ref, cached_ref, values_ref)):
        rows_ref[...] = ref[...].reshape(TILES * LANES, LANES).astype(F32)
        for u in range(YU):
            for r in range(XR):
                if part == 1:
                    tile = rows_ref[pl.ds(u * XR * LANES + r, LANES, stride=XR), :]
                else:
                    tile = rows_ref[pl.ds(r * YU * LANES + u, LANES, stride=YU), :]
                send_ref[pl.ds(part * TILES + u * XR + r, LANES, stride=SEND), :] = tile.T
    out_ref[...] = send_ref[...].astype(BF16)


def softmax_kernel(
    query_x_ref, key_x_ref, query_y_ref, key_y_ref,
    kernel_x_ref, kernel_xt_ref, kernel_y_ref, low_y_ref,
    tiled_qx_ref, tiled_kx_ref, tiled_qy_ref, tiled_ky_ref,
    rows_ref,
):
    head = lax.axis_index("slab") // HEAD
    source = lax.broadcasted_iota(jnp.int32, (LANES, LANES), 0)
    lane = lax.broadcasted_iota(jnp.int32, (LANES, LANES), 1)
    spread = (source == head * HEAD + lane % HEAD).astype(BF16)

    def permuted(ref, step):
        rows_ref[0 : step * LANES, :] = ref[...].astype(F32)
        return jnp.concatenate(
            [rows_ref[pl.ds(r, LANES, stride=step), :] for r in range(step)], axis=0
        ).astype(BF16)

    def softmax(tiled_q, tiled_k):
        first = lax.broadcasted_iota(jnp.int32, tiled_q.shape, 1) < HEAD
        scores = dot(jnp.where(first, tiled_q, 0), tiled_k, ((1,), (1,))) / ROOT
        top = jnp.max(scores, axis=1, keepdims=True)
        power = jnp.exp(scores - top)
        return power / jnp.sum(power, axis=1, keepdims=True)

    tiled_qx = dot(permuted(query_x_ref, XR), spread).astype(BF16)
    tiled_kx = dot(permuted(key_x_ref, XR), spread).astype(BF16)
    tiled_qy = dot(permuted(query_y_ref, YU), spread).astype(BF16)
    tiled_ky = dot(permuted(key_y_ref, YU), spread).astype(BF16)
    kernel_x = softmax(tiled_qx, tiled_kx)
    kernel_y = softmax(tiled_qy, tiled_ky)
    kernel_x_ref[...] = kernel_x
    kernel_xt_ref[...] = kernel_x.T.astype(BF16)
    kernel_y_ref[...] = kernel_y
    low_y_ref[...] = kernel_y.astype(BF16)
    tiled_qx_ref[...] = tiled_qx
    tiled_kx_ref[...] = tiled_kx
    tiled_qy_ref[...] = tiled_qy
    tiled_ky_ref[...] = tiled_ky


def channel_kernel(
    field_ref,
    kernel_x_ref, kernel_xt_ref, kernel_y_ref, low_y_ref,
    tiled_qx_ref, tiled_kx_ref, tiled_qy_ref, tiled_ky_ref,
    out_ref, rows_ref, back_ref,
):
    rows_ref[...] = field_ref[...].astype(F32)

    def tile(q):
        return rows_ref[pl.ds(q, LANES, stride=SEND), :].astype(BF16)

    def field(part):
        return jnp.concatenate(
            [
                jnp.concatenate([tile(part * TILES + u * XR + r) for u in range(YU)], axis=1)
                for r in range(XR)
            ],
            axis=0,
        )

    grad = field(0)
    values = field(2)
    cached = jnp.concatenate(
        [
            jnp.concatenate([tile(TILES + u * XR + r) for r in range(XR)], axis=1)
            for u in range(YU)
        ],
        axis=0,
    )
    mixed = dot(kernel_xt_ref[...], grad).astype(BF16)
    grad_values = dot(mixed, low_y_ref[...])
    for u in range(YU):
        for r in range(XR):
            back_ref[pl.ds(u * XR + r, LANES, stride=BACK), :] = grad_values[
                r * LANES : (r + 1) * LANES, u * LANES : (u + 1) * LANES
            ]

    def factor_grads(kernel, coupling, tiled_q, tiled_k):
        delta = jnp.sum(kernel * coupling, axis=1, keepdims=True)
        weighted = kernel * (coupling - delta) / ROOT
        high = weighted.astype(BF16)
        low = (weighted - high.astype(F32)).astype(BF16)
        grad_query = dot(high, tiled_k) + dot(low, tiled_k)
        grad_key = dot(high, tiled_q, ((0,), (0,))) + dot(low, tiled_q, ((0,), (0,)))
        return grad_query, grad_key

    query_x, key_x = factor_grads(
        kernel_x_ref[...], dot(grad, cached), tiled_qx_ref[...], tiled_kx_ref[...]
    )
    query_y, key_y = factor_grads(
        kernel_y_ref[...], dot(mixed, values, ((0,), (0,))), tiled_qy_ref[...], tiled_ky_ref[...]
    )
    slots = [query_x[r * LANES : (r + 1) * LANES] for r in range(XR)]
    slots += [key_x[r * LANES : (r + 1) * LANES] for r in range(XR)]
    slots += [query_y[u * LANES : (u + 1) * LANES] for u in range(YU)]
    slots += [key_y[u * LANES : (u + 1) * LANES] for u in range(YU)]
    group = lax.broadcasted_iota(jnp.int32, (LANES, LANES), 1) // HEAD
    for line in range(4):
        total = jnp.zeros((LANES, LANES), F32)
        for place, slot in enumerate(slots[line * 4 : line * 4 + 4]):
            total = jnp.where(group == place, slot, total)
        back_ref[pl.ds(TILES + line, LANES, stride=BACK), :] = total
    out_ref[...] = back_ref[...].astype(BF16)


def unpack_kernel(
    back_ref, values_ref, query_x_ref, key_x_ref, query_y_ref, key_y_ref, rows_ref, frame_ref
):
    rows_ref[...] = back_ref[...].astype(F32)
    for u in range(YU):
        for r in range(XR):
            tile = rows_ref[pl.ds(u * XR + r, LANES, stride=BACK), :]
            frame_ref[pl.ds(r * YU * LANES + u, LANES, stride=YU), :] = tile.T
    values_ref[...] = frame_ref[...].astype(BF16).reshape(values_ref.shape)
    source = lax.broadcasted_iota(jnp.int32, (LANES, 4 * LANES), 0)
    lane = lax.broadcasted_iota(jnp.int32, (LANES, 4 * LANES), 1)
    spread = (source == (lane // LANES) * HEAD + lane % HEAD).astype(BF16)
    own = source // HEAD == (lane % LANES) // HEAD
    sums = []
    for line in range(3):
        shares = rows_ref[pl.ds(TILES + line, LANES, stride=BACK), :].astype(BF16)
        total = jnp.sum(jnp.where(own, dot(shares, spread), 0.0), axis=0, keepdims=True)
        sums += [total[:, k * LANES : (k + 1) * LANES] for k in range(4)]
    for r in range(XR):
        query_x_ref[r : r + 1, :] = sums[r]
        key_x_ref[r : r + 1, :] = sums[XR + r]
    for u in range(YU):
        query_y_ref[u : u + 1, :] = sums[2 * XR + u]
        key_y_ref[u : u + 1, :] = sums[2 * XR + YU + u]


def shape(*dims, dtype=F32):
    return jax.ShapeDtypeStruct(dims, dtype)


def exchange(rows, count):
    parts = rows.reshape(LANES, count // 2, 2, LANES)
    moved = lax.all_to_all(parts, "slab", split_axis=0, concat_axis=0, tiled=True)
    return moved.reshape(LANES * count, LANES)


def on_device(grad_out, cached, values, query_x, key_x, query_y, key_y):
    nx, ny = XR * LANES, YU * LANES
    packed = pl.pallas_call(
        pack_kernel,
        out_shape=shape(SEND * LANES, LANES, dtype=BF16),
        scratch_shapes=[pltpu.VMEM((TILES * LANES, LANES), F32), pltpu.VMEM((SEND * LANES, LANES), F32)],
    )(grad_out, cached.transpose(1, 0, 2), values)
    fields = exchange(packed, SEND)
    kernels = pl.pallas_call(
        softmax_kernel,
        out_shape=(
            shape(nx, nx),
            shape(nx, nx, dtype=BF16),
            shape(ny, ny),
            shape(ny, ny, dtype=BF16),
            shape(nx, LANES, dtype=BF16),
            shape(nx, LANES, dtype=BF16),
            shape(ny, LANES, dtype=BF16),
            shape(ny, LANES, dtype=BF16),
        ),
        scratch_shapes=[pltpu.VMEM((ny, LANES), F32)],
    )(query_x, key_x, query_y, key_y)
    back = pl.pallas_call(
        channel_kernel,
        out_shape=shape(BACK * LANES, LANES, dtype=BF16),
        scratch_shapes=[pltpu.VMEM((SEND * LANES, LANES), F32), pltpu.VMEM((BACK * LANES, LANES), F32)],
    )(fields, *kernels)
    shares = exchange(back, BACK)
    return pl.pallas_call(
        unpack_kernel,
        out_shape=(
            shape(XR, ny, LANES, dtype=BF16),
            shape(XR, LANES),
            shape(XR, LANES),
            shape(YU, LANES),
            shape(YU, LANES),
        ),
        scratch_shapes=[pltpu.VMEM((BACK * LANES, LANES), F32), pltpu.VMEM((TILES * LANES, LANES), F32)],
    )(shares)


def solution(mesh):
    return jax.shard_map(
        on_device,
        mesh=mesh,
        in_specs=(
            P(("traj", "slab"), None, None),
            P("traj", "slab", None),
            P(("traj", "slab"), None, None),
            P("traj", None),
            P("traj", None),
            P("traj", None),
            P("traj", None),
        ),
        out_specs=(
            P(("traj", "slab"), None, None),
            P(("traj", "slab"), None),
            P(("traj", "slab"), None),
            P(("traj", "slab"), None),
            P(("traj", "slab"), None),
        ),
        check_vma=False,
    )
```

time: 827 us -> 72.5 us (0.09)
  blocking collectives: 486 us -> 22.2 us
  waiting for transfers between devices: 206 us -> 19.2 us
  matrix products: 37.6 us -> 0 us
  local copies, waits for them, and re-layouts: 35.5 us -> 0.82 us
  between operations: 15.8 us -> 0.64 us
  other arithmetic: 13.5 us -> 0 us
  starting transfers between devices: 30.7 us -> 18.4 us
  Pallas kernels: 0 us -> 10.8 us
    psum x1 -> x0, blocking collectives: 486 us -> none  [on_device(): x_delta_total = lax.psum(jnp.stack(delta_terms), 'slab')]
    unnamed x2 -> x0, waiting for transfers between devices: 192 us -> none
    dot_general x56 -> x0, matrix products: 37.6 us -> none  [the longest x8 7.55 us: local_terms(): jnp.dot(weighted, key_rows.astype(jnp.float32), precision=lax.Precision.H...]
    unnamed x90 -> x2, local copies, waits for them, and re-layouts: 24.8 us -> 0.82 us
    all_to_all x0 -> x1, blocking collectives: none -> 22.2 us  [exchange(): lax.all_to_all(parts, 'slab', split_axis=0, concat_axis=0, tiled=True)]
    all_to_all x2 -> x1, starting transfers between devices: 30.5 us -> 18.4 us  [exchange(): lax.all_to_all(parts, 'slab', split_axis=0, concat_axis=0, tiled=True)]
    pallas_call x0 -> x4, Pallas kernels: none -> 10.8 us  [the longest x1 3.84 us: on_device(): pl.pallas_call(channel_kernel, out_shape=shape(BACK * LANES, LANES, dtype...]
    all_to_all x2 -> x1, waiting for transfers between devices: 13.2 us -> 19.2 us  [exchange(): lax.all_to_all(parts, 'slab', split_axis=0, concat_axis=0, tiled=True)]
  transfers between devices with their start and end apart: 3 -> 1, of which waited for: 3 -> 1; matrix products, arithmetic and copies ran while one was open for 1% -> 0% of each run, Pallas kernels for 0% -> 4%
where the time goes in v1:
time: 72.5 us; the launch traced here: 72.2 us
  blocking collectives  22.2 us (31%)
  waiting for transfers between devices  19.2 us (26%)
  starting transfers between devices  18.4 us (25%)
  Pallas kernels  10.8 us (15%)
  local copies, waits for them, and re-layouts  0.82 us (1%)
    all_to_all x1, blocking collectives, exchange(): lax.all_to_all(parts, 'slab', split_axis=0, concat_axis=0, tiled=True)  22.2 us
    all_to_all x1, waiting for transfers between devices, exchange(): lax.all_to_all(parts, 'slab', split_axis=0, concat_axis=0, tiled=True)  19.2 us
    all_to_all x1, starting transfers between devices, exchange(): lax.all_to_all(parts, 'slab', split_axis=0, concat_axis=0, tiled=True)  18.4 us
    pallas_call x1, Pallas kernels, on_device(): pl.pallas_call(channel_kernel, out_shape=shape(BACK * LANES, LANES, dtype...  3.84 us
    pallas_call x1, Pallas kernels, on_device(): pl.pallas_call(softmax_kernel, out_shape=(shape(nx, nx), shape(nx, nx, dt...  2.72 us
    pallas_call x1, Pallas kernels, on_device(): pl.pallas_call(pack_kernel, out_shape=shape(SEND * LANES, LANES, dtype=BF...  2.37 us
    pallas_call x1, Pallas kernels, on_device(): pl.pallas_call(unpack_kernel, out_shape=(shape(XR, ny, LANES, dtype=BF16)...  1.9 us
  transfers between devices with their start and end apart: 1, of which 1 were waited for; matrix products, arithmetic and copies ran while one was open for 0% of the time, Pallas kernels for 4%

profile of v1, /device:TPU:1, one launch (start us, length us, event | category | flops | bytes accessed | tf_op | source)
XLA Modules:
  0.0 72.2 jit_solution(2814917510600464256)
XLA Ops:
  0.6 2.4 %shard_map.110 = bf16[2304,128]{1,0:T(8,128)(2,1)} custom-call(bf16[2,384,128]{2,1,0:T(8,128)(2,1)} %grad_ref.1, bf16[3,256,128]{2,1,0:T(8,128)(2,1)} %bitcast.9, bf16[2,384,128]{2,1,0:T(8,128)(2,1)} %values_ref.1), custom_call_target="tpu_custom_call" | custom-call | tf_op jit(solution)/shard_map/pallas_call | solution.py:183
  3.0 18.4 %all-to-all-start = ((bf16[128,9,2,128]{3,2,1,0:T(2,128)(2,1)}), bf16[128,9,2,128]{3,2,1,0:T(2,128)(2,1)S(1)}, u32[]{:S(2)}, u32[]{:S(2)}) async-start(bf16[128,9,2,128]{3,2,1,0:T(2,128)(2,1)} %bitcast.6), calls=%async_computation | async-start | bytes 1179648 | tf_op jit(solution)/shard_map/all_to_all | solution.py:177
  21.4 2.7 %shard_map.111 = (f32[256,256]{1,0:T(8,128)}, bf16[256,256]{1,0:T(8,128)(2,1)}, f32[384,384]{1,0:T(8,128)}, bf16[384,384]{1,0:T(8,128)(2,1)}, bf16[256,128]{1,0:...) custom-call(bf16[256,128]{1,0:T(8,128)(2,1)} %query_x_ref.1, ...), custom_call_target="tpu_custom_call" | custom-call | tf_op jit(solution)/shard_map/pallas_call | solution.py:189
  24.1 19.2 %all-to-all-done = bf16[128,9,2,128]{3,2,1,0:T(2,128)(2,1)S(1)} async-done(((bf16[128,9,2,128]{3,2,1,0:T(2,128)(2,1)}), bf16[128,9,2,128]{3,2,1,0:T(2,128)(2,1)S(1)}, u32[]{:S(2)}, u32[]{:S(2)}) %all-to-all-start) | async-done | bytes 589856 | tf_op jit(solution)/shard_map/all_to_all | solution.py:177
  43.4 0.0 copy-start
  43.4 0.8 %copy-done = bf16[128,9,2,128]{3,2,1,0:T(2,128)(2,1)} copy-done((bf16[128,9,2,128]{3,2,1,0:T(2,128)(2,1)}, bf16[128,9,2,128]{3,2,1,0:T(2,128)(2,1)S(1)}, u32[]{:S(2)}) %copy-start) | copy-done | bytes 589848
  44.2 3.8 %shard_map.112 = bf16[1280,128]{1,0:T(8,128)(2,1)} custom-call(bf16[2304,128]{1,0:T(8,128)(2,1)} %bitcast.5, f32[256,256]{1,0:T(8,128)} %get-tuple-element.13.kernel_x_ref, bf16[256,256]{1,0:T(8,128)(2,1)} %get-tuple-element.14.kernel_xt_ref, f32[384,384]{1,0:T(8,128)} %get-tuple-element.15.kernel_y_ref, bf16[384,384]{1,0:T(8,128)(2,1)} %get-tuple-element.16.low_y_ref, ...), custom_call_target="tpu_custom_call" | custom-call | tf_op jit(solution)/shard_map/pallas_call | solution.py:203
  48.0 22.2 %all_to_all.10 = bf16[128,5,2,128]{3,2,1,0:T(2,128)(2,1)} all-to-all(bf16[128,5,2,128]{3,2,1,0:T(2,128)(2,1)} %bitcast.7), channel_id=1, replica_groups=mesh['traj'=4,'slab'=128] {'slab'}, dimensions={0} | all-to-all | bytes 655360 | tf_op jit(solution)/shard_map/all_to_all | solution.py:177
  70.3 1.9 %shard_map.113 = (bf16[2,384,128]{2,1,0:T(8,128)(2,1)}, f32[2,128]{1,0:T(2,128)}, f32[2,128]{1,0:T(2,128)}, f32[3,128]{1,0:T(4,128)}, f32[3,128]{1,0:T(4,128)}) custom-call(bf16[1280,128]{1,0:T(8,128)(2,1)} %bitcast.8), custom_call_target="tpu_custom_call" | custom-call | tf_op jit(solution)/shard_map/pallas_call | solution.py:209
Async XLA Ops:
  3.0 40.4 %all-to-all-start = ((bf16[128,9,2,128]{3,2,1,0:T(2,128)(2,1)}), bf16[128,9,2,128]{3,2,1,0:T(2,128)(2,1)S(1)}, u32[]{:S(2)}, u32[]{:S(2)}) async-start(bf16[128,9,2,128]{3,2,1,0:T(2,128)(2,1)} %bitcast.6), calls=%async_computation | async-start | bytes 1179648 | tf_op jit(solution)/shard_map/all_to_all | solution.py:177
  43.4 0.8 %copy-start = (bf16[128,9,2,128]{3,2,1,0:T(2,128)(2,1)}, bf16[128,9,2,128]{3,2,1,0:T(2,128)(2,1)S(1)}, u32[]{:S(2)}) copy-start(bf16[128,9,2,128]{3,2,1,0:T(2,128)(2,1)S(1)} %all-to-all-done) | copy-start | bytes 1769476

commit v2 on v1

--- a/solution.py
+++ b/solution.py
@@ -172,6 +172,10 @@
     return jax.ShapeDtypeStruct(dims, dtype)
 
 
+def on_chip(array):
+    return pltpu.with_memory_space_constraint(array, pltpu.VMEM)
+
+
 def exchange(rows, count):
     parts = rows.reshape(LANES, count // 2, 2, LANES)
     moved = lax.all_to_all(parts, "slab", split_axis=0, concat_axis=0, tiled=True)
@@ -182,29 +186,29 @@
     nx, ny = XR * LANES, YU * LANES
     packed = pl.pallas_call(
         pack_kernel,
-        out_shape=shape(SEND * LANES, LANES, dtype=BF16),
+        out_shape=pltpu.VMEM((SEND * LANES, LANES), BF16),
         scratch_shapes=[pltpu.VMEM((TILES * LANES, LANES), F32), pltpu.VMEM((SEND * LANES, LANES), F32)],
     )(grad_out, cached.transpose(1, 0, 2), values)
     fields = exchange(packed, SEND)
     kernels = pl.pallas_call(
         softmax_kernel,
         out_shape=(
-            shape(nx, nx),
-            shape(nx, nx, dtype=BF16),
-            shape(ny, ny),
-            shape(ny, ny, dtype=BF16),
-            shape(nx, LANES, dtype=BF16),
-            shape(nx, LANES, dtype=BF16),
-            shape(ny, LANES, dtype=BF16),
-            shape(ny, LANES, dtype=BF16),
+            pltpu.VMEM((nx, nx), F32),
+            pltpu.VMEM((nx, nx), BF16),
+            pltpu.VMEM((ny, ny), F32),
+            pltpu.VMEM((ny, ny), BF16),
+            pltpu.VMEM((nx, LANES), BF16),
+            pltpu.VMEM((nx, LANES), BF16),
+            pltpu.VMEM((ny, LANES), BF16),
+            pltpu.VMEM((ny, LANES), BF16),
         ),
         scratch_shapes=[pltpu.VMEM((ny, LANES), F32)],
     )(query_x, key_x, query_y, key_y)
     back = pl.pallas_call(
         channel_kernel,
-        out_shape=shape(BACK * LANES, LANES, dtype=BF16),
+        out_shape=pltpu.VMEM((BACK * LANES, LANES), BF16),
         scratch_shapes=[pltpu.VMEM((SEND * LANES, LANES), F32), pltpu.VMEM((BACK * LANES, LANES), F32)],
-    )(fields, *kernels)
+    )(*map(on_chip, (fields, *kernels)))
     shares = exchange(back, BACK)
     return pl.pallas_call(
         unpack_kernel,
@@ -216,7 +220,7 @@
             shape(YU, LANES),
         ),
         scratch_shapes=[pltpu.VMEM((BACK * LANES, LANES), F32), pltpu.VMEM((TILES * LANES, LANES), F32)],
-    )(shares)
+    )(on_chip(shares))
 
 
 def solution(mesh):

time: 72.5 us -> 68 us (0.938)
  Pallas kernels: 10.8 us -> 6.64 us
  waiting for transfers between devices: 19.2 us -> 20.2 us
  local copies, waits for them, and re-layouts: 0.82 us -> 0 us
    pallas_call x3, Pallas kernels: 8.93 us -> 5.7 us  [the longest x1 2.36 us: on_device(): pl.pallas_call(pack_kernel, out_shape=pltpu.VMEM((SEND * LANES, LANES), B...]
    pallas_call x1, Pallas kernels: 1.9 us -> 0.94 us  [on_device(): pl.pallas_call(unpack_kernel, out_shape=(shape(XR, ny, LANES, dtype=BF16)...]
    all_to_all x1, waiting for transfers between devices: 19.2 us -> 20.2 us  [exchange(): lax.all_to_all(parts, 'slab', split_axis=0, concat_axis=0, tiled=True)]
    unnamed x2 -> x0, local copies, waits for them, and re-layouts: 0.82 us -> none
  transfers between devices with their start and end apart: 1 -> 1, of which waited for: 1 -> 1; matrix products, arithmetic and copies ran while one was open for 0% -> 0% of each run, Pallas kernels for 4% -> 3%
where the time goes in v2:
time: 68 us; the launch traced here: 67.7 us
  blocking collectives  21.8 us (32%)
  waiting for transfers between devices  20.2 us (30%)
  starting transfers between devices  18.4 us (27%)
  Pallas kernels  6.64 us (10%)
    all_to_all x1, blocking collectives, exchange(): lax.all_to_all(parts, 'slab', split_axis=0, concat_axis=0, tiled=True)  21.8 us
    all_to_all x1, waiting for transfers between devices, exchange(): lax.all_to_all(parts, 'slab', split_axis=0, concat_axis=0, tiled=True)  20.2 us
    all_to_all x1, starting transfers between devices, exchange(): lax.all_to_all(parts, 'slab', split_axis=0, concat_axis=0, tiled=True)  18.4 us
    pallas_call x1, Pallas kernels, on_device(): pl.pallas_call(pack_kernel, out_shape=pltpu.VMEM((SEND * LANES, LANES), B...  2.36 us
    pallas_call x1, Pallas kernels, on_device(): pl.pallas_call(softmax_kernel, out_shape=(pltpu.VMEM((nx, nx), F32), pltp...  1.77 us
    pallas_call x1, Pallas kernels, on_device(): pl.pallas_call(channel_kernel, out_shape=pltpu.VMEM((BACK * LANES, LANES)...  1.56 us
  transfers between devices with their start and end apart: 1, of which 1 were waited for; matrix products, arithmetic and copies ran while one was open for 0% of the time, Pallas kernels for 3%

profile of v2, /device:TPU:1, one launch (start us, length us, event | category | flops | bytes accessed | tf_op | source)
XLA Modules:
  0.0 67.7 jit_solution(11627512248060694604)
XLA Ops:
  0.6 2.4 %shard_map.110 = bf16[2304,128]{1,0:T(8,128)(2,1)} custom-call(bf16[2,384,128]{2,1,0:T(8,128)(2,1)} %grad_ref.1, bf16[3,256,128]{2,1,0:T(8,128)(2,1)} %bitcast.8, bf16[2,384,128]{2,1,0:T(8,128)(2,1)} %values_ref.1), custom_call_target="tpu_custom_call" | custom-call | tf_op jit(solution)/shard_map/pallas_call | solution.py:187
  3.0 18.4 %all-to-all-start = ((bf16[128,9,2,128]{3,2,1,0:T(2,128)(2,1)}), bf16[128,9,2,128]{3,2,1,0:T(2,128)(2,1)S(1)}, u32[]{:S(2)}, u32[]{:S(2)}) async-start(bf16[128,9,2,128]{3,2,1,0:T(2,128)(2,1)} %bitcast.1), calls=%async_computation | async-start | bytes 1179648 | tf_op jit(solution)/shard_map/all_to_all | solution.py:181
  21.4 1.8 %shard_map.111 = (f32[256,256]{1,0:T(8,128)S(1)}, bf16[256,256]{1,0:T(8,128)(2,1)S(1)}, f32[384,384]{1,0:T(8,128)S(1)}, bf16[384,384]{1,0:T(8,128)(2,1)S(1)}, bf...) custom-call(bf16[256,128]{1,0:T(8,128)(2,1)} %query_x_ref.1, ...), custom_call_target="tpu_custom_call" | custom-call | tf_op jit(solution)/shard_map/pallas_call | solution.py:193
  23.2 20.2 %all-to-all-done = bf16[128,9,2,128]{3,2,1,0:T(2,128)(2,1)S(1)} async-done(((bf16[128,9,2,128]{3,2,1,0:T(2,128)(2,1)}), bf16[128,9,2,128]{3,2,1,0:T(2,128)(2,1)S(1)}, u32[]{:S(2)}, u32[]{:S(2)}) %all-to-all-start) | async-done | bytes 589856 | tf_op jit(solution)/shard_map/all_to_all | solution.py:181
  43.4 1.6 %shard_map.112 = bf16[1280,128]{1,0:T(8,128)(2,1)S(1)} custom-call(bf16[2304,128]{1,0:T(8,128)(2,1)S(1)} %bitcast.5, f32[256,256]{1,0:T(8,128)S(1)} %get-tuple-element.13.kernel_x_ref, bf16[256,256]{1,0:T(8,128)(2,1)S(1)} %get-tuple-element.14.kernel_xt_ref, f32[384,384]{1,0:T(8,128)S(1)} %get-tuple-element.15.kernel_y_ref, ...), custom_call_target="tpu_custom_call" | custom-call | tf_op jit(solution)/shard_map/pallas_call | solution.py:207
  45.0 21.8 %all_to_all.10 = bf16[128,5,2,128]{3,2,1,0:T(2,128)(2,1)S(1)} all-to-all(bf16[128,5,2,128]{3,2,1,0:T(2,128)(2,1)S(1)} %bitcast.6), channel_id=1, replica_groups=mesh['traj'=4,'slab'=128] {'slab'}, dimensions={0} | all-to-all | bytes 655360 | tf_op jit(solution)/shard_map/all_to_all | solution.py:181
  66.8 0.9 %shard_map.113 = (bf16[2,384,128]{2,1,0:T(8,128)(2,1)}, f32[2,128]{1,0:T(2,128)}, f32[2,128]{1,0:T(2,128)}, f32[3,128]{1,0:T(4,128)}, f32[3,128]{1,0:T(4,128)}) custom-call(bf16[1280,128]{1,0:T(8,128)(2,1)S(1)} %bitcast.7), custom_call_target="tpu_custom_call" | custom-call | tf_op jit(solution)/shard_map/pallas_call | solution.py:213
Async XLA Ops:
  3.0 40.4 %all-to-all-start = ((bf16[128,9,2,128]{3,2,1,0:T(2,128)(2,1)}), bf16[128,9,2,128]{3,2,1,0:T(2,128)(2,1)S(1)}, u32[]{:S(2)}, u32[]{:S(2)}) async-start(bf16[128,9,2,128]{3,2,1,0:T(2,128)(2,1)} %bitcast.1), calls=%async_computation | async-start | bytes 1179648 | tf_op jit(solution)/shard_map/all_to_all | solution.py:181

commit v3 on v2

--- a/solution.py
+++ b/solution.py
@@ -15,6 +15,7 @@
 TILES = XR * YU
 SEND = 3 * TILES
 BACK = TILES + 4
+Z, Y, CORES = 8, 8, 2
 F32 = jnp.float32
 BF16 = jnp.bfloat16
 ROOT = math.sqrt(HEAD)
@@ -22,6 +23,16 @@
 
 def dot(a, b, dims=((1,), (0,))):
     return lax.dot_general(a, b, (dims, ((), ())), preferred_element_type=F32)
+
+
+def owner(p):
+    z, core, y = Z - 1 - p // (Y * CORES), CORES - 1 - p // Y % CORES, Y - 1 - p % Y
+    return (z * Y + y) * CORES + core
+
+
+def place(s):
+    z, y, core = s // (Y * CORES), s // CORES % Y, s % CORES
+    return ((Z - 1 - z) * CORES + CORES - 1 - core) * Y + Y - 1 - y
 
 
 def pack_kernel(grad_ref, cached_ref, values_ref, out_ref, rows_ref, send_ref):
@@ -40,13 +51,20 @@
 def softmax_kernel(
     query_x_ref, key_x_ref, query_y_ref, key_y_ref,
     kernel_x_ref, kernel_xt_ref, kernel_y_ref, low_y_ref,
-    tiled_qx_ref, tiled_kx_ref, tiled_qy_ref, tiled_ky_ref,
+    tiled_qx_ref, tiled_kx_ref, tiled_qy_ref, tiled_ky_ref, natural_ref, placed_ref,
     rows_ref,
 ):
-    head = lax.axis_index("slab") // HEAD
+    head = place(lax.axis_index("slab")) // HEAD
     source = lax.broadcasted_iota(jnp.int32, (LANES, LANES), 0)
     lane = lax.broadcasted_iota(jnp.int32, (LANES, LANES), 1)
     spread = (source == head * HEAD + lane % HEAD).astype(BF16)
+
+    natural = (source == owner(lane)).astype(BF16)
+    placed = (owner(source) == lane).astype(BF16)
+
+    def put(rows):
+        blocks = [dot(placed, rows[i : i + LANES]) for i in range(0, rows.shape[0], LANES)]
+        return jnp.concatenate(blocks, axis=0).astype(BF16)
 
     def permuted(ref, step):
         rows_ref[0 : step * LANES, :] = ref[...].astype(F32)
@@ -61,26 +79,28 @@
         power = jnp.exp(scores - top)
         return power / jnp.sum(power, axis=1, keepdims=True)
 
-    tiled_qx = dot(permuted(query_x_ref, XR), spread).astype(BF16)
+    tiled_qx = dot(put(permuted(query_x_ref, XR)), spread).astype(BF16)
     tiled_kx = dot(permuted(key_x_ref, XR), spread).astype(BF16)
     tiled_qy = dot(permuted(query_y_ref, YU), spread).astype(BF16)
     tiled_ky = dot(permuted(key_y_ref, YU), spread).astype(BF16)
     kernel_x = softmax(tiled_qx, tiled_kx)
     kernel_y = softmax(tiled_qy, tiled_ky)
     kernel_x_ref[...] = kernel_x
-    kernel_xt_ref[...] = kernel_x.T.astype(BF16)
+    kernel_xt_ref[...] = put(kernel_x.T.astype(BF16))
     kernel_y_ref[...] = kernel_y
     low_y_ref[...] = kernel_y.astype(BF16)
     tiled_qx_ref[...] = tiled_qx
     tiled_kx_ref[...] = tiled_kx
     tiled_qy_ref[...] = tiled_qy
     tiled_ky_ref[...] = tiled_ky
+    natural_ref[...] = natural
+    placed_ref[...] = placed
 
 
 def channel_kernel(
     field_ref,
     kernel_x_ref, kernel_xt_ref, kernel_y_ref, low_y_ref,
-    tiled_qx_ref, tiled_kx_ref, tiled_qy_ref, tiled_ky_ref,
+    tiled_qx_ref, tiled_kx_ref, tiled_qy_ref, tiled_ky_ref, natural_ref, placed_ref,
     out_ref, rows_ref, back_ref,
 ):
     rows_ref[...] = field_ref[...].astype(F32)
@@ -99,12 +119,10 @@
 
     grad = field(0)
     values = field(2)
+    cached = jnp.concatenate([tile(TILES + q) for q in range(TILES)], axis=1)
+    cached = dot(natural_ref[...], cached).astype(BF16)
     cached = jnp.concatenate(
-        [
-            jnp.concatenate([tile(TILES + u * XR + r) for r in range(XR)], axis=1)
-            for u in range(YU)
-        ],
-        axis=0,
+        [cached[:, u * XR * LANES : (u + 1) * XR * LANES] for u in range(YU)], axis=0
     )
     mixed = dot(kernel_xt_ref[...], grad).astype(BF16)
     grad_values = dot(mixed, low_y_ref[...])
@@ -129,16 +147,24 @@
     query_y, key_y = factor_grads(
         kernel_y_ref[...], dot(mixed, values, ((0,), (0,))), tiled_qy_ref[...], tiled_ky_ref[...]
     )
-    slots = [query_x[r * LANES : (r + 1) * LANES] for r in range(XR)]
-    slots += [key_x[r * LANES : (r + 1) * LANES] for r in range(XR)]
+    group = lax.broadcasted_iota(jnp.int32, (LANES, LANES), 1) // HEAD
+
+    def line_up(slots):
+        total = jnp.zeros((LANES, LANES), F32)
+        for at, slot in slots:
+            total = jnp.where(group == at, slot, total)
+        return total
+
+    slots = [key_x[r * LANES : (r + 1) * LANES] for r in range(XR)]
     slots += [query_y[u * LANES : (u + 1) * LANES] for u in range(YU)]
     slots += [key_y[u * LANES : (u + 1) * LANES] for u in range(YU)]
-    group = lax.broadcasted_iota(jnp.int32, (LANES, LANES), 1) // HEAD
-    for line in range(4):
-        total = jnp.zeros((LANES, LANES), F32)
-        for place, slot in enumerate(slots[line * 4 : line * 4 + 4]):
-            total = jnp.where(group == place, slot, total)
-        back_ref[pl.ds(TILES + line, LANES, stride=BACK), :] = total
+    lines = [line_up(zip((2, 3), slots[:2])), line_up(zip(range(4), slots[2:6])), line_up(zip((0, 1), slots[6:]))]
+    lines = dot(placed_ref[...], jnp.concatenate(lines, axis=1).astype(BF16))
+    first = line_up((r, query_x[r * LANES : (r + 1) * LANES]) for r in range(XR))
+    back_ref[pl.ds(TILES, LANES, stride=BACK), :] = first + lines[:, :LANES]
+    back_ref[pl.ds(TILES + 1, LANES, stride=BACK), :] = lines[:, LANES : 2 * LANES]
+    back_ref[pl.ds(TILES + 2, LANES, stride=BACK), :] = lines[:, 2 * LANES :]
+    back_ref[pl.ds(TILES + 3, LANES, stride=BACK), :] = jnp.zeros((LANES, LANES), F32)
     out_ref[...] = back_ref[...].astype(BF16)
 
 
@@ -178,7 +204,10 @@
 
 def exchange(rows, count):
     parts = rows.reshape(LANES, count // 2, 2, LANES)
-    moved = lax.all_to_all(parts, "slab", split_axis=0, concat_axis=0, tiled=True)
+    order = [[owner(p) for p in range(LANES)]]
+    moved = lax.all_to_all(
+        parts, "slab", split_axis=0, concat_axis=0, tiled=True, axis_index_groups=order
+    )
     return moved.reshape(LANES * count, LANES)
 
 
@@ -201,6 +230,8 @@
             pltpu.VMEM((nx, LANES), BF16),
             pltpu.VMEM((ny, LANES), BF16),
             pltpu.VMEM((ny, LANES), BF16),
+            pltpu.VMEM((LANES, LANES), BF16),
+            pltpu.VMEM((LANES, LANES), BF16),
         ),
         scratch_shapes=[pltpu.VMEM((ny, LANES), F32)],
     )(query_x, key_x, query_y, key_y)

time: 68 us -> 63.3 us (0.931)
  waiting for transfers between devices: 20.2 us -> 14.8 us
    all_to_all x1, waiting for transfers between devices: 20.2 us -> 14.8 us  [exchange(): lax.all_to_all(parts, 'slab', split_axis=0, concat_axis=0, tiled=True, ax...]
where the time goes in v3:
time: 63.3 us; the launch traced here: 63.1 us
  blocking collectives  21.7 us (34%)
  starting transfers between devices  19 us (30%)
  waiting for transfers between devices  14.8 us (23%)
  Pallas kernels  6.97 us (11%)
  between operations  0.66 us (1%)
    all_to_all x1, blocking collectives, exchange(): lax.all_to_all(parts, 'slab', split_axis=0, concat_axis=0, tiled=True, ax...  21.7 us
    all_to_all x1, starting transfers between devices, exchange(): lax.all_to_all(parts, 'slab', split_axis=0, concat_axis=0, tiled=True, ax...  19 us
    all_to_all x1, waiting for transfers between devices, exchange(): lax.all_to_all(parts, 'slab', split_axis=0, concat_axis=0, tiled=True, ax...  14.8 us
    pallas_call x1, Pallas kernels, on_device(): pl.pallas_call(pack_kernel, out_shape=pltpu.VMEM((SEND * LANES, LANES), B...  2.36 us
    pallas_call x1, Pallas kernels, on_device(): pl.pallas_call(softmax_kernel, out_shape=(pltpu.VMEM((nx, nx), F32), pltp...  1.94 us
    pallas_call x1, Pallas kernels, on_device(): pl.pallas_call(channel_kernel, out_shape=pltpu.VMEM((BACK * LANES, LANES)...  1.73 us
  transfers between devices with their start and end apart: 1, of which 1 were waited for; matrix products, arithmetic and copies ran while one was open for 0% of the time, Pallas kernels for 3%

profile of v3, /device:TPU:1, one launch (start us, length us, event | category | flops | bytes accessed | tf_op | source)
XLA Modules:
  0.0 63.1 jit_solution(15160883850873426367)
XLA Ops:
  0.6 2.4 %shard_map.110 = bf16[2304,128]{1,0:T(8,128)(2,1)} custom-call(bf16[2,384,128]{2,1,0:T(8,128)(2,1)} %grad_ref.1, bf16[3,256,128]{2,1,0:T(8,128)(2,1)} %bitcast.8, bf16[2,384,128]{2,1,0:T(8,128)(2,1)} %values_ref.1), custom_call_target="tpu_custom_call" | custom-call | tf_op jit(solution)/shard_map/pallas_call | solution.py:216
  3.0 19.0 %all-to-all-start = ((bf16[128,9,2,128]{3,2,1,0:T(2,128)(2,1)}), bf16[128,9,2,128]{3,2,1,0:T(2,128)(2,1)S(1)}, u32[]{:S(2)}, u32[]{:S(2)}) async-start(bf16[128,9,2,128]{3,2,1,0:T(2,128)(2,1)} %bitcast.1), calls=%async_computation | async-start | bytes 1179648 | tf_op jit(solution)/shard_map/all_to_all | solution.py:208
  22.0 1.9 %shard_map.111 = (f32[256,256]{1,0:T(8,128)S(1)}, bf16[256,256]{1,0:T(8,128)(2,1)S(1)}, f32[384,384]{1,0:T(8,128)S(1)}, bf16[384,384]{1,0:T(8,128)(2,1)S(1)}, bf...) custom-call(bf16[256,128]{1,0:T(8,128)(2,1)} %query_x_ref.1, ...), custom_call_target="tpu_custom_call" | custom-call | tf_op jit(solution)/shard_map/pallas_call | solution.py:222
  24.0 14.8 %all-to-all-done = bf16[128,9,2,128]{3,2,1,0:T(2,128)(2,1)S(1)} async-done(((bf16[128,9,2,128]{3,2,1,0:T(2,128)(2,1)}), bf16[128,9,2,128]{3,2,1,0:T(2,128)(2,1)S(1)}, u32[]{:S(2)}, u32[]{:S(2)}) %all-to-all-start) | async-done | bytes 589856 | tf_op jit(solution)/shard_map/all_to_all | solution.py:208
  38.7 1.7 %shard_map.112 = bf16[1280,128]{1,0:T(8,128)(2,1)S(1)} custom-call(bf16[2304,128]{1,0:T(8,128)(2,1)S(1)} %bitcast.5, f32[256,256]{1,0:T(8,128)S(1)} %get-tuple-element.15.kernel_x_ref, bf16[256,256]{1,0:T(8,128)(2,1)S(1)} %get-tuple-element.16.kernel_xt_ref, f32[384,384]{1,0:T(8,128)S(1)} %get-tuple-element.17.kernel_y_ref, ...), custom_call_target="tpu_custom_call" | custom-call | tf_op jit(solution)/shard_map/pallas_call | solution.py:238
  40.5 21.7 %all_to_all.10 = bf16[128,5,2,128]{3,2,1,0:T(2,128)(2,1)S(1)} all-to-all(bf16[128,5,2,128]{3,2,1,0:T(2,128)(2,1)S(1)} %bitcast.6), channel_id=1, replica_groups={{127,125,123,121,119,117,115,113,126,124,122,120,118,116,114,112,111,10..., dimensions={0} | all-to-all | bytes 655360 | tf_op jit(solution)/shard_map/all_to_all | solution.py:208
  62.1 0.9 %shard_map.113 = (bf16[2,384,128]{2,1,0:T(8,128)(2,1)}, f32[2,128]{1,0:T(2,128)}, f32[2,128]{1,0:T(2,128)}, f32[3,128]{1,0:T(4,128)}, f32[3,128]{1,0:T(4,128)}) custom-call(bf16[1280,128]{1,0:T(8,128)(2,1)S(1)} %bitcast.7), custom_call_target="tpu_custom_call" | custom-call | tf_op jit(solution)/shard_map/pallas_call | solution.py:244
Async XLA Ops:
  3.0 35.7 %all-to-all-start = ((bf16[128,9,2,128]{3,2,1,0:T(2,128)(2,1)}), bf16[128,9,2,128]{3,2,1,0:T(2,128)(2,1)S(1)}, u32[]{:S(2)}, u32[]{:S(2)}) async-start(bf16[128,9,2,128]{3,2,1,0:T(2,128)(2,1)} %bitcast.1), calls=%async_computation | async-start | bytes 1179648 | tf_op jit(solution)/shard_map/all_to_all | solution.py:208

commit v4 on v3

--- a/solution.py
+++ b/solution.py
@@ -16,6 +16,7 @@
 SEND = 3 * TILES
 BACK = TILES + 4
 Z, Y, CORES = 8, 8, 2
+FIRST = (5, 4)
 F32 = jnp.float32
 BF16 = jnp.bfloat16
 ROOT = math.sqrt(HEAD)
@@ -26,13 +27,15 @@
 
 
 def owner(p):
-    z, core, y = Z - 1 - p // (Y * CORES), CORES - 1 - p // Y % CORES, Y - 1 - p % Y
-    return (z * Y + y) * CORES + core
+    z = (Z + FIRST[0] - p // (Y * CORES)) % Z
+    y = (Y + FIRST[1] - p % Y) % Y
+    return (z * Y + y) * CORES + CORES - 1 - p // Y % CORES
 
 
 def place(s):
-    z, y, core = s // (Y * CORES), s // CORES % Y, s % CORES
-    return ((Z - 1 - z) * CORES + CORES - 1 - core) * Y + Y - 1 - y
+    z = (Z + FIRST[0] - s // (Y * CORES)) % Z
+    y = (Y + FIRST[1] - s // CORES % Y) % Y
+    return (z * CORES + CORES - 1 - s % CORES) * Y + y
 
 
 def pack_kernel(grad_ref, cached_ref, values_ref, out_ref, rows_ref, send_ref):

time: 63.3 us -> 62 us (0.979)
  waiting for transfers between devices: 14.8 us -> 11.8 us
  starting transfers between devices: 19 us -> 20.9 us
    all_to_all x1, waiting for transfers between devices: 14.8 us -> 11.8 us  [exchange(): lax.all_to_all(parts, 'slab', split_axis=0, concat_axis=0, tiled=True, ax...]
    all_to_all x1, starting transfers between devices: 19 us -> 20.9 us  [exchange(): lax.all_to_all(parts, 'slab', split_axis=0, concat_axis=0, tiled=True, ax...]
where the time goes in v4:
time: 62 us; the launch traced here: 61.7 us
  blocking collectives  21.3 us (34%)
  starting transfers between devices  20.9 us (34%)
  waiting for transfers between devices  11.8 us (19%)
  Pallas kernels  7 us (11%)
  between operations  0.66 us (1%)
    all_to_all x1, blocking collectives, exchange(): lax.all_to_all(parts, 'slab', split_axis=0, concat_axis=0, tiled=True, ax...  21.3 us
    all_to_all x1, starting transfers between devices, exchange(): lax.all_to_all(parts, 'slab', split_axis=0, concat_axis=0, tiled=True, ax...  20.9 us
    all_to_all x1, waiting for transfers between devices, exchange(): lax.all_to_all(parts, 'slab', split_axis=0, concat_axis=0, tiled=True, ax...  11.8 us
    pallas_call x1, Pallas kernels, on_device(): pl.pallas_call(pack_kernel, out_shape=pltpu.VMEM((SEND * LANES, LANES), B...  2.36 us
    pallas_call x1, Pallas kernels, on_device(): pl.pallas_call(softmax_kernel, out_shape=(pltpu.VMEM((nx, nx), F32), pltp...  1.97 us
    pallas_call x1, Pallas kernels, on_device(): pl.pallas_call(channel_kernel, out_shape=pltpu.VMEM((BACK * LANES, LANES)...  1.73 us
  transfers between devices with their start and end apart: 1, of which 1 were waited for; matrix products, arithmetic and copies ran while one was open for 0% of the time, Pallas kernels for 3%

profile of v4, /device:TPU:1, one launch (start us, length us, event | category | flops | bytes accessed | tf_op | source)
XLA Modules:
  0.0 61.7 jit_solution(8116649394178633690)
XLA Ops:
  0.6 2.4 %shard_map.110 = bf16[2304,128]{1,0:T(8,128)(2,1)} custom-call(bf16[2,384,128]{2,1,0:T(8,128)(2,1)} %grad_ref.1, bf16[3,256,128]{2,1,0:T(8,128)(2,1)} %bitcast.8, bf16[2,384,128]{2,1,0:T(8,128)(2,1)} %values_ref.1), custom_call_target="tpu_custom_call" | custom-call | tf_op jit(solution)/shard_map/pallas_call | solution.py:219
  3.0 20.9 %all-to-all-start = ((bf16[128,9,2,128]{3,2,1,0:T(2,128)(2,1)}), bf16[128,9,2,128]{3,2,1,0:T(2,128)(2,1)S(1)}, u32[]{:S(2)}, u32[]{:S(2)}) async-start(bf16[128,9,2,128]{3,2,1,0:T(2,128)(2,1)} %bitcast.1), calls=%async_computation | async-start | bytes 1179648 | tf_op jit(solution)/shard_map/all_to_all | solution.py:211
  23.9 2.0 %shard_map.111 = (f32[256,256]{1,0:T(8,128)S(1)}, bf16[256,256]{1,0:T(8,128)(2,1)S(1)}, f32[384,384]{1,0:T(8,128)S(1)}, bf16[384,384]{1,0:T(8,128)(2,1)S(1)}, bf...) custom-call(bf16[256,128]{1,0:T(8,128)(2,1)} %query_x_ref.1, ...), custom_call_target="tpu_custom_call" | custom-call | tf_op jit(solution)/shard_map/pallas_call | solution.py:225
  25.9 11.8 %all-to-all-done = bf16[128,9,2,128]{3,2,1,0:T(2,128)(2,1)S(1)} async-done(((bf16[128,9,2,128]{3,2,1,0:T(2,128)(2,1)}), bf16[128,9,2,128]{3,2,1,0:T(2,128)(2,1)S(1)}, u32[]{:S(2)}, u32[]{:S(2)}) %all-to-all-start) | async-done | bytes 589856 | tf_op jit(solution)/shard_map/all_to_all | solution.py:211
  37.7 1.7 %shard_map.112 = bf16[1280,128]{1,0:T(8,128)(2,1)S(1)} custom-call(bf16[2304,128]{1,0:T(8,128)(2,1)S(1)} %bitcast.5, f32[256,256]{1,0:T(8,128)S(1)} %get-tuple-element.15.kernel_x_ref, bf16[256,256]{1,0:T(8,128)(2,1)S(1)} %get-tuple-element.16.kernel_xt_ref, f32[384,384]{1,0:T(8,128)S(1)} %get-tuple-element.17.kernel_y_ref, ...), custom_call_target="tpu_custom_call" | custom-call | tf_op jit(solution)/shard_map/pallas_call | solution.py:241
  39.5 21.3 %all_to_all.10 = bf16[128,5,2,128]{3,2,1,0:T(2,128)(2,1)S(1)} all-to-all(bf16[128,5,2,128]{3,2,1,0:T(2,128)(2,1)S(1)} %bitcast.6), channel_id=1, replica_groups={{89,87,85,83,81,95,93,91,88,86,84,82,80,94,92,90,73,71,69,67,65,79,77,7..., dimensions={0} | all-to-all | bytes 655360 | tf_op jit(solution)/shard_map/all_to_all | solution.py:211
  60.8 0.9 %shard_map.113 = (bf16[2,384,128]{2,1,0:T(8,128)(2,1)}, f32[2,128]{1,0:T(2,128)}, f32[2,128]{1,0:T(2,128)}, f32[3,128]{1,0:T(4,128)}, f32[3,128]{1,0:T(4,128)}) custom-call(bf16[1280,128]{1,0:T(8,128)(2,1)S(1)} %bitcast.7), custom_call_target="tpu_custom_call" | custom-call | tf_op jit(solution)/shard_map/pallas_call | solution.py:247
Async XLA Ops:
  3.0 34.7 %all-to-all-start = ((bf16[128,9,2,128]{3,2,1,0:T(2,128)(2,1)}), bf16[128,9,2,128]{3,2,1,0:T(2,128)(2,1)S(1)}, u32[]{:S(2)}, u32[]{:S(2)}) async-start(bf16[128,9,2,128]{3,2,1,0:T(2,128)(2,1)} %bitcast.1), calls=%async_computation | async-start | bytes 1179648 | tf_op jit(solution)/shard_map/all_to_all | solution.py:211

commit v5 on v4

--- a/solution.py
+++ b/solution.py
@@ -38,72 +38,56 @@
     return (z * CORES + CORES - 1 - s % CORES) * Y + y
 
 
-def pack_kernel(grad_ref, cached_ref, values_ref, out_ref, rows_ref, send_ref):
+def entry_kernel(
+    grad_ref, cached_ref, values_ref, query_x_ref, key_x_ref, query_y_ref, key_y_ref,
+    out_ref, tiled_qx_ref, tiled_kx_ref, placed_kx_ref, tiled_qy_ref, tiled_ky_ref, natural_ref, placed_ref,
+    rows_ref, send_ref, factor_ref,
+):
     for part, ref in enumerate((grad_ref, cached_ref, values_ref)):
-        rows_ref[...] = ref[...].reshape(TILES * LANES, LANES).astype(F32)
+        rows_ref[part] = ref[...].reshape(TILES * LANES, LANES).astype(F32)
         for u in range(YU):
             for r in range(XR):
                 if part == 1:
-                    tile = rows_ref[pl.ds(u * XR * LANES + r, LANES, stride=XR), :]
+                    tile = rows_ref[part, pl.ds(u * XR * LANES + r, LANES, stride=XR), :]
                 else:
-                    tile = rows_ref[pl.ds(r * YU * LANES + u, LANES, stride=YU), :]
+                    tile = rows_ref[part, pl.ds(r * YU * LANES + u, LANES, stride=YU), :]
                 send_ref[pl.ds(part * TILES + u * XR + r, LANES, stride=SEND), :] = tile.T
     out_ref[...] = send_ref[...].astype(BF16)
 
-
-def softmax_kernel(
-    query_x_ref, key_x_ref, query_y_ref, key_y_ref,
-    kernel_x_ref, kernel_xt_ref, kernel_y_ref, low_y_ref,
-    tiled_qx_ref, tiled_kx_ref, tiled_qy_ref, tiled_ky_ref, natural_ref, placed_ref,
-    rows_ref,
-):
     head = place(lax.axis_index("slab")) // HEAD
     source = lax.broadcasted_iota(jnp.int32, (LANES, LANES), 0)
     lane = lax.broadcasted_iota(jnp.int32, (LANES, LANES), 1)
     spread = (source == head * HEAD + lane % HEAD).astype(BF16)
-
-    natural = (source == owner(lane)).astype(BF16)
     placed = (owner(source) == lane).astype(BF16)
-
-    def put(rows):
-        blocks = [dot(placed, rows[i : i + LANES]) for i in range(0, rows.shape[0], LANES)]
-        return jnp.concatenate(blocks, axis=0).astype(BF16)
-
-    def permuted(ref, step):
-        rows_ref[0 : step * LANES, :] = ref[...].astype(F32)
-        return jnp.concatenate(
-            [rows_ref[pl.ds(r, LANES, stride=step), :] for r in range(step)], axis=0
-        ).astype(BF16)
-
-    def softmax(tiled_q, tiled_k):
-        first = lax.broadcasted_iota(jnp.int32, tiled_q.shape, 1) < HEAD
-        scores = dot(jnp.where(first, tiled_q, 0), tiled_k, ((1,), (1,))) / ROOT
-        top = jnp.max(scores, axis=1, keepdims=True)
-        power = jnp.exp(scores - top)
-        return power / jnp.sum(power, axis=1, keepdims=True)
-
-    tiled_qx = dot(put(permuted(query_x_ref, XR)), spread).astype(BF16)
-    tiled_kx = dot(permuted(key_x_ref, XR), spread).astype(BF16)
-    tiled_qy = dot(permuted(query_y_ref, YU), spread).astype(BF16)
-    tiled_ky = dot(permuted(key_y_ref, YU), spread).astype(BF16)
-    kernel_x = softmax(tiled_qx, tiled_kx)
-    kernel_y = softmax(tiled_qy, tiled_ky)
-    kernel_x_ref[...] = kernel_x
-    kernel_xt_ref[...] = put(kernel_x.T.astype(BF16))
-    kernel_y_ref[...] = kernel_y
-    low_y_ref[...] = kernel_y.astype(BF16)
-    tiled_qx_ref[...] = tiled_qx
-    tiled_kx_ref[...] = tiled_kx
-    tiled_qy_ref[...] = tiled_qy
-    tiled_ky_ref[...] = tiled_ky
-    natural_ref[...] = natural
+    natural_ref[...] = (source == owner(lane)).astype(BF16)
     placed_ref[...] = placed
 
+    def tiled(at, ref, step):
+        factor_ref[at, 0 : step * LANES, :] = dot(ref[...], spread)
+        blocks = [factor_ref[at, pl.ds(r, LANES, stride=step), :] for r in range(step)]
+        return [block.astype(BF16) for block in blocks]
+
+    def put(blocks):
+        return jnp.concatenate([dot(placed, block) for block in blocks], axis=0).astype(BF16)
+
+    query_x = tiled(0, query_x_ref, XR)
+    key_x = tiled(1, key_x_ref, XR)
+    tiled_qx_ref[...] = put(query_x)
+    placed_kx_ref[...] = put(key_x)
+    tiled_kx_ref[...] = jnp.concatenate(key_x, axis=0)
+    tiled_qy_ref[...] = jnp.concatenate(tiled(2, query_y_ref, YU), axis=0)
+    tiled_ky_ref[...] = jnp.concatenate(tiled(3, key_y_ref, YU), axis=0)
+
+
+def softmax(tiled_q, tiled_k, axis):
+    first = lax.broadcasted_iota(jnp.int32, tiled_q.shape, 1) < HEAD
+    scores = dot(jnp.where(first, tiled_q, 0), tiled_k, ((1,), (1,))) / ROOT
+    power = jnp.exp(scores - jnp.max(scores, axis=axis, keepdims=True))
+    return power / jnp.sum(power, axis=axis, keepdims=True)
+
 
 def channel_kernel(
-    field_ref,
-    kernel_x_ref, kernel_xt_ref, kernel_y_ref, low_y_ref,
-    tiled_qx_ref, tiled_kx_ref, tiled_qy_ref, tiled_ky_ref, natural_ref, placed_ref,
+    field_ref, tiled_qx_ref, tiled_kx_ref, placed_kx_ref, tiled_qy_ref, tiled_ky_ref, natural_ref, placed_ref,
     out_ref, rows_ref, back_ref,
 ):
     rows_ref[...] = field_ref[...].astype(F32)
@@ -127,8 +111,11 @@
     cached = jnp.concatenate(
         [cached[:, u * XR * LANES : (u + 1) * XR * LANES] for u in range(YU)], axis=0
     )
-    mixed = dot(kernel_xt_ref[...], grad).astype(BF16)
-    grad_values = dot(mixed, low_y_ref[...])
+    kernel_x = softmax(tiled_qx_ref[...], tiled_kx_ref[...], 1)
+    kernel_xt = softmax(placed_kx_ref[...], tiled_qx_ref[...], 0)
+    kernel_y = softmax(tiled_qy_ref[...], tiled_ky_ref[...], 1)
+    mixed = dot(kernel_xt.astype(BF16), grad).astype(BF16)
+    grad_values = dot(mixed, kernel_y.astype(BF16))
     for u in range(YU):
         for r in range(XR):
             back_ref[pl.ds(u * XR + r, LANES, stride=BACK), :] = grad_values[
@@ -145,10 +132,10 @@
         return grad_query, grad_key
 
     query_x, key_x = factor_grads(
-        kernel_x_ref[...], dot(grad, cached), tiled_qx_ref[...], tiled_kx_ref[...]
+        kernel_x, dot(grad, cached), tiled_qx_ref[...], tiled_kx_ref[...]
     )
     query_y, key_y = factor_grads(
-        kernel_y_ref[...], dot(mixed, values, ((0,), (0,))), tiled_qy_ref[...], tiled_ky_ref[...]
+        kernel_y, dot(mixed, values, ((0,), (0,))), tiled_qy_ref[...], tiled_ky_ref[...]
     )
     group = lax.broadcasted_iota(jnp.int32, (LANES, LANES), 1) // HEAD
 
@@ -216,19 +203,11 @@
 
 def on_device(grad_out, cached, values, query_x, key_x, query_y, key_y):
     nx, ny = XR * LANES, YU * LANES
-    packed = pl.pallas_call(
-        pack_kernel,
-        out_shape=pltpu.VMEM((SEND * LANES, LANES), BF16),
-        scratch_shapes=[pltpu.VMEM((TILES * LANES, LANES), F32), pltpu.VMEM((SEND * LANES, LANES), F32)],
-    )(grad_out, cached.transpose(1, 0, 2), values)
-    fields = exchange(packed, SEND)
-    kernels = pl.pallas_call(
-        softmax_kernel,
+    packed, *factors = pl.pallas_call(
+        entry_kernel,
         out_shape=(
-            pltpu.VMEM((nx, nx), F32),
-            pltpu.VMEM((nx, nx), BF16),
-            pltpu.VMEM((ny, ny), F32),
-            pltpu.VMEM((ny, ny), BF16),
+            pltpu.VMEM((SEND * LANES, LANES), BF16),
+            pltpu.VMEM((nx, LANES), BF16),
             pltpu.VMEM((nx, LANES), BF16),
             pltpu.VMEM((nx, LANES), BF16),
             pltpu.VMEM((ny, LANES), BF16),
@@ -236,13 +215,18 @@
             pltpu.VMEM((LANES, LANES), BF16),
             pltpu.VMEM((LANES, LANES), BF16),
         ),
-        scratch_shapes=[pltpu.VMEM((ny, LANES), F32)],
-    )(query_x, key_x, query_y, key_y)
+        scratch_shapes=[
+            pltpu.VMEM((3, TILES * LANES, LANES), F32),
+            pltpu.VMEM((SEND * LANES, LANES), F32),
+            pltpu.VMEM((4, ny, LANES), F32),
+        ],
+    )(grad_out, cached.transpose(1, 0, 2), values, query_x, key_x, query_y, key_y)
+    fields = exchange(packed, SEND)
     back = pl.pallas_call(
         channel_kernel,
         out_shape=pltpu.VMEM((BACK * LANES, LANES), BF16),
         scratch_shapes=[pltpu.VMEM((SEND * LANES, LANES), F32), pltpu.VMEM((BACK * LANES, LANES), F32)],
-    )(*map(on_chip, (fields, *kernels)))
+    )(*map(on_chip, (fields, *factors)))
     shares = exchange(back, BACK)
     return pl.pallas_call(
         unpack_kernel,

time: 62 us -> 61.6 us (level)
  blocking collectives: 21.3 us -> 55.8 us
  starting transfers between devices: 20.9 us -> 0 us
  waiting for transfers between devices: 11.8 us -> 0 us
  Pallas kernels: 7 us -> 4.96 us
    all_to_all x1 -> x2, blocking collectives: 21.3 us -> 55.8 us  [exchange(): lax.all_to_all(parts, 'slab', split_axis=0, concat_axis=0, tiled=True, ax...]
    all_to_all x1 -> x0, starting transfers between devices: 20.9 us -> none  [exchange(): lax.all_to_all(parts, 'slab', split_axis=0, concat_axis=0, tiled=True, ax...]
    all_to_all x1 -> x0, waiting for transfers between devices: 11.8 us -> none  [exchange(): lax.all_to_all(parts, 'slab', split_axis=0, concat_axis=0, tiled=True, ax...]
    pallas_call x2 -> x1, Pallas kernels: 4.33 us -> 1.8 us  [on_device(): pl.pallas_call(entry_kernel, out_shape=(pltpu.VMEM((SEND * LANES, LANES),...]
  transfers between devices with their start and end apart: 1 -> 0, of which waited for: 1 -> 0; matrix products, arithmetic and copies ran while one was open for 0% -> 0% of each run, Pallas kernels for 3% -> 0%
where the time goes in v5:
time: 61.6 us; the launch traced here: 61.4 us
  blocking collectives  55.8 us (91%)
  Pallas kernels  4.96 us (8%)
  between operations  0.65 us (1%)
    all_to_all x2, blocking collectives, exchange(): lax.all_to_all(parts, 'slab', split_axis=0, concat_axis=0, tiled=True, ax...  55.8 us
    pallas_call x1, Pallas kernels, on_device(): pl.pallas_call(channel_kernel, out_shape=pltpu.VMEM((BACK * LANES, LANES)...  2.23 us
    pallas_call x1, Pallas kernels, on_device(): pl.pallas_call(entry_kernel, out_shape=(pltpu.VMEM((SEND * LANES, LANES),...  1.8 us

profile of v5, /device:TPU:1, one launch (start us, length us, event | category | flops | bytes accessed | tf_op | source)
XLA Modules:
  0.0 61.4 jit_solution(5018153239907711009)
XLA Ops:
  0.6 1.8 %shard_map.110 = (bf16[2304,128]{1,0:T(8,128)(2,1)S(1)}, bf16[256,128]{1,0:T(8,128)(2,1)S(1)}, bf16[256,128]{1,0:T(8,128)(2,1)S(1)}, bf16[256,128]{1,0:T(8,128)(...) custom-call(bf16[2,384,128]{2,1,0:T(8,128)(2,1)} %grad_ref.1, ...), custom_call_target="tpu_custom_call" | custom-call | tf_op jit(solution)/shard_map/pallas_call | solution.py:206
  2.4 34.5 %all_to_all.10 = bf16[128,9,2,128]{3,2,1,0:T(2,128)(2,1)S(1)} all-to-all(bf16[128,9,2,128]{3,2,1,0:T(2,128)(2,1)S(1)} %bitcast.8), channel_id=1, replica_groups={{89,87,85,83,81,95,93,91,88,86,84,82,80,94,92,90,73,71,69,67,65,79,77,7..., dimensions={0} | all-to-all | bytes 1179648 | tf_op jit(solution)/shard_map/all_to_all | solution.py:198
  37.0 2.2 %shard_map.111 = bf16[1280,128]{1,0:T(8,128)(2,1)S(1)} custom-call(bf16[2304,128]{1,0:T(8,128)(2,1)S(1)} %bitcast.5, bf16[256,128]{1,0:T(8,128)(2,1)S(1)} %get-tuple-element.14.tiled_qx_ref, bf16[256,128]{1,0:T(8,128)(2,1)S(1)} %get-tuple-element.15.tiled_kx_ref, bf16[256,128]{1,0:T(8,128)(2,1)S(1)} %get-tuple-element.16.placed_kx_ref, ...), custom_call_target="tpu_custom_call" | custom-call | tf_op jit(solution)/shard_map/pallas_call | solution.py:225
  39.2 21.3 %all_to_all.11 = bf16[128,5,2,128]{3,2,1,0:T(2,128)(2,1)S(1)} all-to-all(bf16[128,5,2,128]{3,2,1,0:T(2,128)(2,1)S(1)} %bitcast.7), channel_id=1, replica_groups={{89,87,85,83,81,95,93,91,88,86,84,82,80,94,92,90,73,71,69,67,65,79,77,7..., dimensions={0} | all-to-all | bytes 655360 | tf_op jit(solution)/shard_map/all_to_all | solution.py:198
  60.5 0.9 %shard_map.112 = (bf16[2,384,128]{2,1,0:T(8,128)(2,1)}, f32[2,128]{1,0:T(2,128)}, f32[2,128]{1,0:T(2,128)}, f32[3,128]{1,0:T(4,128)}, f32[3,128]{1,0:T(4,128)}) custom-call(bf16[1280,128]{1,0:T(8,128)(2,1)S(1)} %bitcast.6), custom_call_target="tpu_custom_call" | custom-call | tf_op jit(solution)/shard_map/pallas_call | solution.py:231

commit v6 on v5

--- a/solution.py
+++ b/solution.py
@@ -128,7 +128,8 @@
         high = weighted.astype(BF16)
         low = (weighted - high.astype(F32)).astype(BF16)
         grad_query = dot(high, tiled_k) + dot(low, tiled_k)
-        grad_key = dot(high, tiled_q, ((0,), (0,))) + dot(low, tiled_q, ((0,), (0,)))
+        turned_q = tiled_q.T
+        grad_key = (dot(turned_q, high) + dot(turned_q, low)).T
         return grad_query, grad_key
 
     query_x, key_x = factor_grads(

time: 61.6 us -> 61.6 us (level)
  no operation moved by 1% of the time
where the time goes in v6:
time: 61.6 us; the launch traced here: 61.5 us
  blocking collectives  55.8 us (91%)
  Pallas kernels  4.97 us (8%)
  between operations  0.65 us (1%)
    all_to_all x2, blocking collectives, exchange(): lax.all_to_all(parts, 'slab', split_axis=0, concat_axis=0, tiled=True, ax...  55.8 us
    pallas_call x1, Pallas kernels, on_device(): pl.pallas_call(channel_kernel, out_shape=pltpu.VMEM((BACK * LANES, LANES)...  2.24 us
    pallas_call x1, Pallas kernels, on_device(): pl.pallas_call(entry_kernel, out_shape=(pltpu.VMEM((SEND * LANES, LANES),...  1.8 us

profile of v6, /device:TPU:1, one launch (start us, length us, event | category | flops | bytes accessed | tf_op | source)
XLA Modules:
  0.0 61.5 jit_solution(3749931184755967283)
XLA Ops:
  0.6 1.8 %shard_map.110 = (bf16[2304,128]{1,0:T(8,128)(2,1)S(1)}, bf16[256,128]{1,0:T(8,128)(2,1)S(1)}, bf16[256,128]{1,0:T(8,128)(2,1)S(1)}, bf16[256,128]{1,0:T(8,128)(...) custom-call(bf16[2,384,128]{2,1,0:T(8,128)(2,1)} %grad_ref.1, ...), custom_call_target="tpu_custom_call" | custom-call | tf_op jit(solution)/shard_map/pallas_call | solution.py:207
  2.4 34.5 %all_to_all.10 = bf16[128,9,2,128]{3,2,1,0:T(2,128)(2,1)S(1)} all-to-all(bf16[128,9,2,128]{3,2,1,0:T(2,128)(2,1)S(1)} %bitcast.8), channel_id=1, replica_groups={{89,87,85,83,81,95,93,91,88,86,84,82,80,94,92,90,73,71,69,67,65,79,77,7..., dimensions={0} | all-to-all | bytes 1179648 | tf_op jit(solution)/shard_map/all_to_all | solution.py:199
  37.0 2.2 %shard_map.111 = bf16[1280,128]{1,0:T(8,128)(2,1)S(1)} custom-call(bf16[2304,128]{1,0:T(8,128)(2,1)S(1)} %bitcast.5, bf16[256,128]{1,0:T(8,128)(2,1)S(1)} %get-tuple-element.14.tiled_qx_ref, bf16[256,128]{1,0:T(8,128)(2,1)S(1)} %get-tuple-element.15.tiled_kx_ref, bf16[256,128]{1,0:T(8,128)(2,1)S(1)} %get-tuple-element.16.placed_kx_ref, ...), custom_call_target="tpu_custom_call" | custom-call | tf_op jit(solution)/shard_map/pallas_call | solution.py:226
  39.2 21.3 %all_to_all.11 = bf16[128,5,2,128]{3,2,1,0:T(2,128)(2,1)S(1)} all-to-all(bf16[128,5,2,128]{3,2,1,0:T(2,128)(2,1)S(1)} %bitcast.7), channel_id=1, replica_groups={{89,87,85,83,81,95,93,91,88,86,84,82,80,94,92,90,73,71,69,67,65,79,77,7..., dimensions={0} | all-to-all | bytes 655360 | tf_op jit(solution)/shard_map/all_to_all | solution.py:199
  60.5 0.9 %shard_map.112 = (bf16[2,384,128]{2,1,0:T(8,128)(2,1)}, f32[2,128]{1,0:T(2,128)}, f32[2,128]{1,0:T(2,128)}, f32[3,128]{1,0:T(4,128)}, f32[3,128]{1,0:T(4,128)}) custom-call(bf16[1280,128]{1,0:T(8,128)(2,1)S(1)} %bitcast.6), custom_call_target="tpu_custom_call" | custom-call | tf_op jit(solution)/shard_map/pallas_call | solution.py:232
